TPU v7x, 32 devices: a whole 2x2x4 slice. The times are simulated.
32 devices in a mesh: slab: 8 (over z, y), sub: 4 (over x, core).
Axes of the slice: x: 2, y: 2, z: 4, core: 2. Of those that a mesh axis runs over, the one named last changes fastest.
Arguments:
- coefficients: bfloat16 [7, 6, 6, 64, 12, 128], P(None, None, None, 'slab', 'sub'), may hold values from -1 to 1
- earlier: float32 [30, 6, 64, 12, 128], P(None, None, 'slab', 'sub'), may hold values from -6 to 6
- start: float32 [6, 64, 12, 128], P(None, 'slab', 'sub'), may hold values from -8 to 8
- shifts: float32 [5], replicated, may hold values from -0.3 to 0.3
Outputs:
- new_basis: float32 [6, 6, 64, 12, 128], P(None, None, 'slab', 'sub')
- projection: float32 [30, 6], replicated
- triangle: float32 [6, 6], replicated
All inputs are finite; a program needn't handle non-finite values.
Results may differ from a plain program's by a relative error of at most 0.0015.
Values may be sent and summed in bfloat16 or wider, within the bound.
A program may use at most 64 MiB of HBM per device.

v0:
```python
import jax
import jax.numpy as jnp
from jax import lax
from jax.sharding import PartitionSpec as P


def padded_2(block, sides, width):
    for axis, dim in sides:
        count = lax.axis_size(axis)
        forward = [(i, i + 1) for i in range(count - 1)]
        backward = [(target, source) for source, target in forward]
        low = lax.ppermute(
            lax.slice_in_dim(block, block.shape[dim] - width, None, axis=dim), axis, forward
        )
        high = lax.ppermute(lax.slice_in_dim(block, 0, width, axis=dim), axis, backward)
        block = jnp.concatenate([low, block, high], axis=dim)
    return block


def nearby_fields(padded):
    center = padded[:, 1:-1, 1:-1]
    zeros_edge = jnp.zeros_like(center[..., :1])
    lower_y = jnp.concatenate([zeros_edge, center[..., :-1]], axis=3)
    upper_y = jnp.concatenate([center[..., 1:], zeros_edge], axis=3)
    return [
        center,
        padded[:, :-2, 1:-1],
        padded[:, 2:, 1:-1],
        padded[:, 1:-1, :-2],
        padded[:, 1:-1, 2:],
        lower_y,
        upper_y,
    ]


def apply_padded(coefficients, padded, theta):
    fields = nearby_fields(padded)
    result = (1.0 - theta) * fields[0]
    for coupling in range(len(fields)):
        result = result + jnp.sum(coefficients[coupling] * fields[coupling][None], axis=1)
    return result


def body(coefficients, earlier, start, shifts):
    depth = shifts.shape[0]
    vectors = [start]
    current = padded_2(start, (("slab", 1),), depth)
    wide_coefficients = padded_2(coefficients, (("slab", 3),), depth)
    for step in range(depth):
        beside = padded_2(current, (("sub", 2),), 1)
        padded = jnp.pad(beside, ((0, 0), (1, 1), (0, 0), (0, 0)))
        current = apply_padded(wide_coefficients, padded, shifts[step])
        vectors.append(current[:, depth:-depth])
    basis = jnp.stack(vectors)
    block_count = basis.shape[0]
    flat = basis.reshape(block_count, -1)
    earlier_flat = earlier.reshape(earlier.shape[0], -1)
    count = flat.shape[1] * lax.axis_size("slab") * lax.axis_size("sub")
    local_cross = jnp.dot(earlier_flat, flat.T, precision=lax.Precision.HIGHEST)
    local_self = jnp.dot(flat, flat.T, precision=lax.Precision.HIGHEST)
    local_earlier = jnp.dot(earlier_flat, earlier_flat.T, precision=lax.Precision.HIGHEST)
    cross_sum, self_sum, earlier_sum = lax.psum(
        (local_cross, local_self, local_earlier), ("slab", "sub")
    )
    projection = cross_sum / count
    rest = flat - jnp.dot(projection.T, earlier_flat, precision=lax.Precision.HIGHEST)
    weighted = jnp.dot(earlier_sum / count, projection, precision=lax.Precision.HIGHEST)
    gram = self_sum / count - 2.0 * jnp.dot(
        projection.T, projection, precision=lax.Precision.HIGHEST
    )
    gram = gram + jnp.dot(projection.T, weighted, precision=lax.Precision.HIGHEST)
    lower = jnp.linalg.cholesky(gram)
    new_flat = lax.linalg.triangular_solve(lower, rest, left_side=True, lower=True)
    return (new_flat.reshape(basis.shape), projection, lower.T)


def solution(mesh):
    placed = (
        P(None, None, None, "slab", "sub", None),
        P(None, None, "slab", "sub", None),
        P(None, "slab", "sub", None),
        P(),
    )
    return jax.shard_map(
        body,
        mesh=mesh,
        in_specs=placed,
        out_specs=(P(None, None, "slab", "sub", None), P(), P()),
        check_vma=False,
    )
```

profile of v0, /device:TPU:0, one launch (start us, length us, event | category | flops | bytes accessed | tf_op | source)
XLA Modules:
  0.0 177.3 jit_solution(12425602278455781404)
XLA Ops:
  0.6 1.0 fusion.71
  1.6 1.3 collective-permute-start.1
  2.9 5.5 %collective-permute-start = (f32[6,5,3,128]{3,1,2,0:T(8,128)S(1)}, f32[6,5,3,128]{3,1,2,0:T(8,128)S(1)}, u32[]{:S(2)}, u32[]{:S(2)}) collective-permute-start(f32[6,5,3,128]{3,1,2,0:T(8,128)S(1)} %get-tuple-element.112), channel_id=1, source_target_pairs={{0,4},{4,8},{8,12},{12,16},{16,20},{20,24},{24,28},{1,5},{5,9},{9,... | collective-permute-start | bytes 138248 | tf_op jit(solution)/shard_map/ppermute | solution.py:12
  8.4 2.5 %fusion.55 = (bf16[7,6,6,5,3,128]{5,3,4,2,1,0:T(8,128)(2,1)S(1)}, bf16[7,6,6,5,3,128]{5,3,4,2,1,0:T(8,128)(2,1)S(1)}) fusion(bf16[7,6,6,8,3,128]{5,3,4,2,1,0:T(8,128)(2,1)} %param.4), kind=kLoop, calls=%fused_computation.150 | loop fusion | bytes 3870720 | tf_op jit(solution)/shard_map/slice | solution.py:13
  10.9 1.5 copy.352
  12.4 1.3 collective-permute-start.3
  13.7 1.5 copy.351
  15.2 6.6 %collective-permute-start.2 = (bf16[7,6,6,5,3,128]{5,0,4,3,2,1:T(8,128)(2,1)}, bf16[7,6,6,5,3,128]{5,0,4,3,2,1:T(8,128)(2,1)}, u32[]{:S(2)}, u32[]{:S(2)}) collective-permute-start(bf16[7,6,6,5,3,128]{5,0,4,3,2,1:T(8,128)(2,1)} %copy.351), channel_id=1, source_target_pairs={{0,4},{4,8},{8,12},{12,16},{16,20},{20,24},{24,28},{1,5},{5,9},{9,... | collective-permute-start | bytes 2903048 | tf_op jit(solution)/shard_map/ppermute | solution.py:12
  21.8 2.3 %fusion.39 = f32[30,30]{1,0:T(8,128)S(1)} fusion(f32[30,6,8,3,128]{4,2,3,1,0:T(8,128)S(1)} %copy-done.1), kind=kOutput, calls=%fused_computation.76 | convolution fusion | flops 199065600 | bytes 2215440 | tf_op jit(solution)/shard_map/dot_general | solution.py:61
  24.9 2.6 %copy.340 = f32[30,6,8,3,128]{4,3,2,1,0:T(4,128)} copy(f32[30,6,8,3,128]{4,2,3,1,0:T(8,128)S(1)} %copy-done.1) | data formatting | bytes 4423680 | tf_op args[1]
  30.8 4.5 %reshape.317 = f32[30,18432]{1,0:T(8,128)} reshape(f32[30,6,8,3,128]{4,3,2,1,0:T(4,128)} %copy.340) | data formatting | bytes 4423680 | tf_op jit(solution)/shard_map/reshape | solution.py:57
  35.4 1.3 collective-permute-start.4
  36.7 1.3 collective-permute-start.5
  38.3 3.3 %collective-permute-done.5 = f32[6,18,1,128]{3,1,2,0:T(8,128)S(1)} collective-permute-done((f32[6,18,1,128]{3,1,2,0:T(8,128)S(1)}, f32[6,18,1,128]{3,1,2,0:T(8,128)S(1)}, u32[]{:S(2)}, u32[]{:S(2)}) %collective-permute-start.5) | collective-permute-done | bytes 55328 | tf_op jit(solution)/shard_map/ppermute | solution.py:15
  41.7 1.6 copy.319
  43.3 21.9 %collective-permute-done.2 = bf16[7,6,6,5,3,128]{5,0,4,3,2,1:T(8,128)(2,1)} collective-permute-done((bf16[7,6,6,5,3,128]{5,0,4,3,2,1:T(8,128)(2,1)}, bf16[7,6,6,5,3,128]{5,0,4,3,2,1:T(8,128)(2,1)}, u32[]{:S(2)}, u32[]{:S(2)}) %collective-permute-start.2) | collective-permute-done | bytes 967712 | tf_op jit(solution)/shard_map/ppermute | solution.py:12
  65.2 1.6 copy.318
  66.8 2.9 %pad_maximum_fusion = bf16[7,6,6,18,3,128]{5,3,4,2,1,0:T(8,128)(2,1)S(1)} fusion(bf16[7,6,6,5,3,128]{5,3,4,2,1,0:T(8,128)(2,1)S(1)} %copy.319, bf16[7,6,6,8,3,128]{5,3,4,2,1,0:T(8,128)(2,1)S(1)} %copy-done.2, bf16[7,6,6,5,3,128]{5,3,4,2,1,0:T(8,128)(2,1)S(1)} %copy.318), kind=kLoop, calls=%fused_computation.1 | loop fusion | flops 10450944 | bytes 6967296 | tf_op jit(solution)/shard_map/concatenate | solution.py:16
  69.7 1.1 fusion.4
  70.8 1.1 copy-done
  72.8 1.9 %collective-permute-start.6 = (f32[6,18,1,128]{3,1,2,0:T(8,128)}, f32[6,18,1,128]{3,1,2,0:T(8,128)S(1)}, u32[]{:S(2)}, u32[]{:S(2)}) collective-permute-start(f32[6,18,1,128]{3,1,2,0:T(8,128)} %get-tuple-element.102), channel_id=1, source_target_pairs={{0,1},{1,2},{2,3},{4,5},{5,6},{6,7},{8,9},{9,10},{10,11},{12,13},{... | collective-permute-start | bytes 165896 | tf_op jit(solution)/shard_map/ppermute | solution.py:12
  74.7 1.5 collective-permute-start.7
  76.2 0.7 stack.43
  77.2 1.7 collective-permute-done.7
  79.1 3.5 %fusion.5 = (f32[6,18,3,128]{3,1,2,0:T(8,128)S(1)}, f32[6,18,3,128]{3,1,2,0:T(8,128)S(1)}, f32[6,18,3,128]{3,1,2,0:T(8,128)S(1)}, f32[6,18,3,128]{3,1,2,0:T(8,12...) fusion(f32[6,18,3,128]{3,1,2,0:T(8,128)S(1)} %add_add_fusion.3, ...), kind=kLoop, calls=%fused_computation.42 | loop fusion | flops 4935168 | bytes 5806080 | tf_op jit(solution)/shard_map/reduce_sum | solution.py:40
  83.5 4.9 %collective-permute-start.8 = (f32[6,18,1,128]{3,1,2,0:T(8,128)}, f32[6,18,1,128]{3,1,2,0:T(8,128)S(1)}, u32[]{:S(2)}, u32[]{:S(2)}) collective-permute-start(f32[6,18,1,128]{3,1,2,0:T(8,128)} %get-tuple-element.96), channel_id=1, source_target_pairs={{0,1},{1,2},{2,3},{4,5},{5,6},{6,7},{8,9},{9,10},{10,11},{12,13},{... | collective-permute-start | bytes 165896 | tf_op jit(solution)/shard_map/ppermute | solution.py:12
  88.4 1.3 collective-permute-start.9
  89.8 0.7 stack.44
  90.7 1.0 collective-permute-done.9
  91.9 3.5 %fusion.6 = (f32[6,18,3,128]{3,1,2,0:T(8,128)S(1)}, f32[6,18,3,128]{3,1,2,0:T(8,128)S(1)}, f32[6,18,3,128]{3,1,2,0:T(8,128)S(1)}, f32[6,18,3,128]{3,1,2,0:T(8,12...) fusion(f32[6,18,3,128]{3,1,2,0:T(8,128)S(1)} %add_add_fusion.2, ...), kind=kLoop, calls=%fused_computation.43 | loop fusion | flops 4935168 | bytes 5806080 | tf_op jit(solution)/shard_map/reduce_sum | solution.py:40
  96.4 4.4 %collective-permute-start.10 = (f32[6,18,1,128]{3,1,2,0:T(8,128)}, f32[6,18,1,128]{3,1,2,0:T(8,128)S(1)}, u32[]{:S(2)}, u32[]{:S(2)}) collective-permute-start(f32[6,18,1,128]{3,1,2,0:T(8,128)} %get-tuple-element.90), channel_id=1, source_target_pairs={{0,1},{1,2},{2,3},{4,5},{5,6},{6,7},{8,9},{9,10},{10,11},{12,13},{... | collective-permute-start | bytes 165896 | tf_op jit(solution)/shard_map/ppermute | solution.py:12
  100.8 1.3 collective-permute-start.11
  102.8 0.7 stack.45
  103.7 1.0 copy.323
  104.8 3.5 %fusion.7 = (f32[6,18,3,128]{3,1,2,0:T(8,128)S(1)}, f32[6,18,3,128]{3,1,2,0:T(8,128)S(1)}, f32[6,18,3,128]{3,1,2,0:T(8,128)S(1)}, f32[6,18,3,128]{3,1,2,0:T(8,12...) fusion(f32[6,18,3,128]{3,1,2,0:T(8,128)S(1)} %add_add_fusion.1, ...), kind=kLoop, calls=%fused_computation.44 | loop fusion | flops 4935168 | bytes 5806080 | tf_op jit(solution)/shard_map/reduce_sum | solution.py:40
  109.3 4.0 %collective-permute-start.12 = (f32[6,18,1,128]{3,1,2,0:T(8,128)}, f32[6,18,1,128]{3,1,2,0:T(8,128)S(1)}, u32[]{:S(2)}, u32[]{:S(2)}) collective-permute-start(f32[6,18,1,128]{3,1,2,0:T(8,128)} %get-tuple-element.84), channel_id=1, source_target_pairs={{0,1},{1,2},{2,3},{4,5},{5,6},{6,7},{8,9},{9,10},{10,11},{12,13},{... | collective-permute-start | bytes 165896 | tf_op jit(solution)/shard_map/ppermute | solution.py:12
  113.3 1.3 collective-permute-start.13
  115.2 0.7 stack.46
  116.1 1.0 copy.324
  117.2 3.5 %fusion.8 = (f32[6,18,3,128]{3,1,2,0:T(8,128)S(1)}, f32[6,18,3,128]{3,1,2,0:T(8,128)S(1)}, f32[6,18,3,128]{3,1,2,0:T(8,128)S(1)}, f32[6,18,3,128]{3,1,2,0:T(8,12...) fusion(f32[6,18,3,128]{3,1,2,0:T(8,128)S(1)} %add_add_fusion, ...), kind=kLoop, calls=%fused_computation.45 | loop fusion | flops 4935168 | bytes 5806080 | tf_op jit(solution)/shard_map/reduce_sum | solution.py:40
  121.0 0.7 stack.41
  121.8 2.2 %fusion.42 = f32[30,6]{0,1:T(8,128)S(1)} fusion(f32[6,6,8,3,128]{4,0,3,2,1:T(8,128)S(1)} %stack.41, f32[30,6,8,3,128]{4,2,3,1,0:T(8,128)S(1)} %copy-done.1), kind=kOutput, calls=%fused_computation.77 | convolution fusion | flops 39813120 | bytes 2654928 | tf_op jit(solution)/shard_map/dot_general | solution.py:59
  124.0 1.4 convolution_bitcast_fusion
  125.5 42.9 %all-reduce.15 = (f32[30,6]{0,1:T(8,128)S(1)}, f32[6,6]{0,1:T(8,128)S(1)}, f32[30,30]{1,0:T(8,128)S(1)}) all-reduce(f32[30,6]{0,1:T(8,128)S(1)} %fusion.42, f32[6,6]{0,1:T(8,128)S(1)} %convolution_bitcast_fusion, f32[30,30]{1,0:T(8,128)S(1)} %fusion.39), channel_id=1, replica_groups=mesh['slab'=8,'sub'=4] {'slab','sub'}, use_global_device_ids=true, to_apply=%region_36.37 | all-reduce | flops 1116 | bytes 8928 | tf_op jit(solution)/shard_map/psum | solution.py:62
  171.3 0.7 stack.48
  172.1 2.9 %convolution_subtract_fusion = f32[6,18432]{1,0:T(8,128)S(1)} fusion(f32[6,18432]{1,0:T(8,128)S(1)} %stack.48, f32[30,6]{0,1:T(8,128)S(1)} %broadcast_multiply_fusion, f32[30,18432]{1,0:T(8,128)} %reshape.317), kind=kOutput, calls=%fused_computation | convolution fusion | flops 39923712 | bytes 3097296 | tf_op jit(solution)/shard_map/dot_general | solution.py:66
  175.0 0.8 fusion.50
  175.7 0.8 copy.342
  (99 shorter events, 11.5 us)
Async XLA Ops:
  1.6 33.7 %collective-permute-start.1 = (f32[6,5,3,128]{3,1,2,0:T(8,128)S(1)}, f32[6,5,3,128]{3,1,2,0:T(8,128)S(1)}, u32[]{:S(2)}, u32[]{:S(2)}) collective-permute-start(f32[6,5,3,128]{3,1,2,0:T(8,128)S(1)} %get-tuple-element.113), channel_id=1, source_target_pairs={{4,0},{8,4},{12,8},{16,12},{20,16},{24,20},{28,24},{5,1},{9,5},{13... | collective-permute-start | bytes 138248 | tf_op jit(solution)/shard_map/ppermute | solution.py:15
  2.9 32.4 %collective-permute-start = (f32[6,5,3,128]{3,1,2,0:T(8,128)S(1)}, f32[6,5,3,128]{3,1,2,0:T(8,128)S(1)}, u32[]{:S(2)}, u32[]{:S(2)}) collective-permute-start(f32[6,5,3,128]{3,1,2,0:T(8,128)S(1)} %get-tuple-element.112), channel_id=1, source_target_pairs={{0,4},{4,8},{8,12},{12,16},{16,20},{20,24},{24,28},{1,5},{5,9},{9,... | collective-permute-start | bytes 138248 | tf_op jit(solution)/shard_map/ppermute | solution.py:12
  12.4 29.3 %collective-permute-start.3 = (bf16[7,6,6,5,3,128]{5,0,4,3,2,1:T(8,128)(2,1)}, bf16[7,6,6,5,3,128]{5,0,4,3,2,1:T(8,128)(2,1)}, u32[]{:S(2)}, u32[]{:S(2)}) collective-permute-start(bf16[7,6,6,5,3,128]{5,0,4,3,2,1:T(8,128)(2,1)} %copy.352), channel_id=1, source_target_pairs={{4,0},{8,4},{12,8},{16,12},{20,16},{24,20},{28,24},{5,1},{9,5},{13... | collective-permute-start | bytes 2903048 | tf_op jit(solution)/shard_map/ppermute | solution.py:15
  13.7 8.1 %copy-start.1 = (f32[30,6,8,3,128]{4,2,3,1,0:T(8,128)S(1)}, f32[30,6,8,3,128]{4,2,3,1,0:T(8,128)}, u32[]{:S(2)}) copy-start(f32[30,6,8,3,128]{4,2,3,1,0:T(8,128)} %param.5) | copy-start | bytes 6635524
  15.2 8.9 %copy-start.9 = (f32[5]{0:T(128)S(1)}, f32[5]{0:T(128)}, u32[]{:S(2)}) copy-start(f32[5]{0:T(128)} %param.7) | copy-start | bytes 64
  15.2 9.6 %copy-start.3 = (f32[6,8,3,128]{3,1,2,0:T(8,128)S(1)}, f32[6,8,3,128]{3,1,2,0:T(8,128)}, u32[]{:S(2)}) copy-start(f32[6,8,3,128]{3,1,2,0:T(8,128)} %param.6) | copy-start | bytes 221188
  15.2 50.0 %collective-permute-start.2 = (bf16[7,6,6,5,3,128]{5,0,4,3,2,1:T(8,128)(2,1)}, bf16[7,6,6,5,3,128]{5,0,4,3,2,1:T(8,128)(2,1)}, u32[]{:S(2)}, u32[]{:S(2)}) collective-permute-start(bf16[7,6,6,5,3,128]{5,0,4,3,2,1:T(8,128)(2,1)} %copy.351), channel_id=1, source_target_pairs={{0,4},{4,8},{8,12},{12,16},{16,20},{20,24},{24,28},{1,5},{5,9},{9,... | collective-permute-start | bytes 2903048 | tf_op jit(solution)/shard_map/ppermute | solution.py:12
  35.4 2.9 %collective-permute-start.4 = (f32[6,18,1,128]{3,1,2,0:T(8,128)S(1)}, f32[6,18,1,128]{3,1,2,0:T(8,128)S(1)}, u32[]{:S(2)}, u32[]{:S(2)}) collective-permute-start(f32[6,18,1,128]{3,1,2,0:T(8,128)S(1)} %get-tuple-element.108), channel_id=1, source_target_pairs={{0,1},{1,2},{2,3},{4,5},{5,6},{6,7},{8,9},{9,10},{10,11},{12,13},{... | collective-permute-start | bytes 165896 | tf_op jit(solution)/shard_map/ppermute | solution.py:12
  36.7 4.9 %collective-permute-start.5 = (f32[6,18,1,128]{3,1,2,0:T(8,128)S(1)}, f32[6,18,1,128]{3,1,2,0:T(8,128)S(1)}, u32[]{:S(2)}, u32[]{:S(2)}) collective-permute-start(f32[6,18,1,128]{3,1,2,0:T(8,128)S(1)} %get-tuple-element.109), channel_id=1, source_target_pairs={{1,0},{2,1},{3,2},{5,4},{6,5},{7,6},{9,8},{10,9},{11,10},{13,12},{... | collective-permute-start | bytes 165896 | tf_op jit(solution)/shard_map/ppermute | solution.py:15
  43.3 23.5 %copy-start.2 = (bf16[7,6,6,8,3,128]{5,3,4,2,1,0:T(8,128)(2,1)S(1)}, bf16[7,6,6,8,3,128]{5,3,4,2,1,0:T(8,128)(2,1)}, u32[]{:S(2)}) copy-start(bf16[7,6,6,8,3,128]{5,3,4,2,1,0:T(8,128)(2,1)} %param.4) | copy-start | bytes 4644868
  69.7 2.2 %copy-start = (bf16[7,6,6,18,3,128]{5,3,4,2,1,0:T(8,128)(2,1)}, bf16[7,6,6,18,3,128]{5,3,4,2,1,0:T(8,128)(2,1)S(1)}, u32[]{:S(2)}) copy-start(bf16[7,6,6,18,3,128]{5,3,4,2,1,0:T(8,128)(2,1)S(1)} %pad_maximum_fusion) | copy-start | bytes 10450948
  72.8 4.4 %collective-permute-start.6 = (f32[6,18,1,128]{3,1,2,0:T(8,128)}, f32[6,18,1,128]{3,1,2,0:T(8,128)S(1)}, u32[]{:S(2)}, u32[]{:S(2)}) collective-permute-start(f32[6,18,1,128]{3,1,2,0:T(8,128)} %get-tuple-element.102), channel_id=1, source_target_pairs={{0,1},{1,2},{2,3},{4,5},{5,6},{6,7},{8,9},{9,10},{10,11},{12,13},{... | collective-permute-start | bytes 165896 | tf_op jit(solution)/shard_map/ppermute | solution.py:12
  74.7 4.3 %collective-permute-start.7 = (f32[6,18,1,128]{3,1,2,0:T(8,128)S(1)}, f32[6,18,1,128]{3,1,2,0:T(8,128)S(1)}, u32[]{:S(2)}, u32[]{:S(2)}) collective-permute-start(f32[6,18,1,128]{3,1,2,0:T(8,128)S(1)} %get-tuple-element.103), channel_id=1, source_target_pairs={{1,0},{2,1},{3,2},{5,4},{6,5},{7,6},{9,8},{10,9},{11,10},{13,12},{... | collective-permute-start | bytes 165896 | tf_op jit(solution)/shard_map/ppermute | solution.py:15
  83.5 7.2 %collective-permute-start.8 = (f32[6,18,1,128]{3,1,2,0:T(8,128)}, f32[6,18,1,128]{3,1,2,0:T(8,128)S(1)}, u32[]{:S(2)}, u32[]{:S(2)}) collective-permute-start(f32[6,18,1,128]{3,1,2,0:T(8,128)} %get-tuple-element.96), channel_id=1, source_target_pairs={{0,1},{1,2},{2,3},{4,5},{5,6},{6,7},{8,9},{9,10},{10,11},{12,13},{... | collective-permute-start | bytes 165896 | tf_op jit(solution)/shard_map/ppermute | solution.py:12
  88.4 3.4 %collective-permute-start.9 = (f32[6,18,1,128]{3,1,2,0:T(8,128)}, f32[6,18,1,128]{3,1,2,0:T(8,128)S(1)}, u32[]{:S(2)}, u32[]{:S(2)}) collective-permute-start(f32[6,18,1,128]{3,1,2,0:T(8,128)} %get-tuple-element.97), channel_id=1, source_target_pairs={{1,0},{2,1},{3,2},{5,4},{6,5},{7,6},{9,8},{10,9},{11,10},{13,12},{... | collective-permute-start | bytes 165896 | tf_op jit(solution)/shard_map/ppermute | solution.py:15
  96.4 8.2 %collective-permute-start.10 = (f32[6,18,1,128]{3,1,2,0:T(8,128)}, f32[6,18,1,128]{3,1,2,0:T(8,128)S(1)}, u32[]{:S(2)}, u32[]{:S(2)}) collective-permute-start(f32[6,18,1,128]{3,1,2,0:T(8,128)} %get-tuple-element.90), channel_id=1, source_target_pairs={{0,1},{1,2},{2,3},{4,5},{5,6},{6,7},{8,9},{9,10},{10,11},{12,13},{... | collective-permute-start | bytes 165896 | tf_op jit(solution)/shard_map/ppermute | solution.py:12
  100.8 3.8 %collective-permute-start.11 = (f32[6,18,1,128]{3,1,2,0:T(8,128)}, f32[6,18,1,128]{3,1,2,0:T(8,128)S(1)}, u32[]{:S(2)}, u32[]{:S(2)}) collective-permute-start(f32[6,18,1,128]{3,1,2,0:T(8,128)} %get-tuple-element.91), channel_id=1, source_target_pairs={{1,0},{2,1},{3,2},{5,4},{6,5},{7,6},{9,8},{10,9},{11,10},{13,12},{... | collective-permute-start | bytes 165896 | tf_op jit(solution)/shard_map/ppermute | solution.py:15
  109.3 7.8 %collective-permute-start.12 = (f32[6,18,1,128]{3,1,2,0:T(8,128)}, f32[6,18,1,128]{3,1,2,0:T(8,128)S(1)}, u32[]{:S(2)}, u32[]{:S(2)}) collective-permute-start(f32[6,18,1,128]{3,1,2,0:T(8,128)} %get-tuple-element.84), channel_id=1, source_target_pairs={{0,1},{1,2},{2,3},{4,5},{5,6},{6,7},{8,9},{9,10},{10,11},{12,13},{... | collective-permute-start | bytes 165896 | tf_op jit(solution)/shard_map/ppermute | solution.py:12
  113.3 3.8 %collective-permute-start.13 = (f32[6,18,1,128]{3,1,2,0:T(8,128)}, f32[6,18,1,128]{3,1,2,0:T(8,128)S(1)}, u32[]{:S(2)}, u32[]{:S(2)}) collective-permute-start(f32[6,18,1,128]{3,1,2,0:T(8,128)} %get-tuple-element.85), channel_id=1, source_target_pairs={{1,0},{2,1},{3,2},{5,4},{6,5},{7,6},{9,8},{10,9},{11,10},{13,12},{... | collective-permute-start | bytes 165896 | tf_op jit(solution)/shard_map/ppermute | solution.py:15
  124.0 47.3 %copy-start.4 = (f32[1,18432]{1,0:T(1,128)S(1)}, f32[1,18432]{1,0:T(1,128)}, u32[]{:S(2)}) copy-start(f32[1,18432]{1,0:T(1,128)} %stack.43) | copy-start | bytes 221188
  124.0 47.3 %copy-start.5 = (f32[1,18432]{1,0:T(1,128)S(1)}, f32[1,18432]{1,0:T(1,128)}, u32[]{:S(2)}) copy-start(f32[1,18432]{1,0:T(1,128)} %stack.44) | copy-start | bytes 221188
  124.0 47.3 %copy-start.6 = (f32[1,18432]{1,0:T(1,128)S(1)}, f32[1,18432]{1,0:T(1,128)}, u32[]{:S(2)}) copy-start(f32[1,18432]{1,0:T(1,128)} %stack.45) | copy-start | bytes 221188
  124.0 47.3 %copy-start.7 = (f32[1,18432]{1,0:T(1,128)S(1)}, f32[1,18432]{1,0:T(1,128)}, u32[]{:S(2)}) copy-start(f32[1,18432]{1,0:T(1,128)} %stack.46) | copy-start | bytes 221188
  168.4 6.5 %copy-start.8 = (f32[30,6]{0,1:T(8,128)}, f32[30,6]{0,1:T(8,128)S(1)}, u32[]{:S(2)}) copy-start(f32[30,6]{0,1:T(8,128)S(1)} %broadcast_multiply_fusion) | copy-start | bytes 2164
where the time goes:
time: 178 us; the launch traced here: 177 us
  blocking collectives  42.9 us (24%)
  starting transfers between devices  37.9 us (21%)
  local copies, waits for them, and re-layouts  32.4 us (18%)
  waiting for transfers between devices  28 us (16%)
  other arithmetic  21.6 us (12%)
  matrix products  9.97 us (6%)
  between operations  4.5 us (3%)
    psum x1, blocking collectives, body(): lax.psum((local_cross, local_self, local_earlier), ('slab', 'sub'))  42.9 us
    ppermute x7, starting transfers between devices, padded_2(): lax.ppermute(lax.slice_in_dim(block, block.shape[dim] - width, None, axis...  28.7 us
    ppermute x7, waiting for transfers between devices, padded_2(): lax.ppermute(lax.slice_in_dim(block, block.shape[dim] - width, None, axis...  21.9 us
    reduce_sum x5, other arithmetic, apply_padded(): jnp.sum(coefficients[coupling] * fields[coupling][None], axis=1)  15.2 us
    ppermute x7, starting transfers between devices, padded_2(): lax.ppermute(lax.slice_in_dim(block, 0, width, axis=dim), axis, backward)  9.21 us
    unnamed x26, local copies, waits for them, and re-layouts  8.24 us
    another operation x18, local copies, waits for them, and re-layouts, body(): basis = jnp.stack(vectors)  8.1 us
    slice x7, local copies, waits for them, and re-layouts, padded_2(): lax.slice_in_dim(block, block.shape[dim] - width, None, axis=dim)  6.15 us
  transfers between devices with their start and end apart: 14, of which 4 were waited for; matrix products, arithmetic and copies ran while one was open for 14% of the time, Pallas kernels for 0%

commit v1 on v0

v1 whole, which is shorter than its diff:
```python
import functools

import jax
import jax.numpy as jnp
from jax import lax
from jax.experimental import pallas as pl
from jax.experimental.pallas import tpu as pltpu
from jax.sharding import PartitionSpec as P

MESH = pl.DeviceIdType.MESH
LANES = 128
ROWS = 8


def dot(a, b, nt=False):
    return lax.dot_general(
        a, b, (((1,), (1 if nt else 0,)), ((), ())),
        precision=lax.Precision.HIGHEST, preferred_element_type=jnp.float32,
    )


def iota(shape, dim):
    return lax.broadcasted_iota(jnp.int32, shape, dim)


def onehot(shape, test):
    return jnp.where(test(iota(shape, 0), iota(shape, 1)), 1.0, 0.0).astype(jnp.float32)


def factors(count):
    found = []
    while count > 1:
        size = max(f for f in range(2, min(count, 8) + 1) if count % f == 0) if any(
            count % f == 0 for f in range(2, min(count, 8) + 1)
        ) else count
        found.append(size)
        count //= size
    return found


def stages_of(sizes):
    found = []
    for axis, count in sizes:
        stride = 1
        for size in factors(count):
            found.append((axis, stride, size))
            stride *= size
    return found


def side_by_side(value):
    count, width = value.shape[0], value.shape[1]
    return jnp.concatenate(
        [value[:, x].reshape(count * ROWS, LANES) for x in range(width)], axis=1
    )


def kernel(
    sizes, coef_hbm, early_hbm, start_hbm, shifts_ref, new_ref, proj_ref, tri_ref,
    coef_in, coef, edge_coef, allv, acc_ref, halo_x, halo_z, send_z, ee, mine, gathered,
    in_sem, halo_send, halo_recv, red_send, red_recv,
):
    depth = shifts_ref.shape[0]
    earlier, comp, width = early_hbm.shape[:3]
    block = depth + 1
    count = comp * width * ROWS * LANES * sizes[0][1] * sizes[1][1]
    stages = stages_of(sizes)
    place = {axis: lax.axis_index(axis) for axis, _ in sizes}
    slab, sub = sizes[0], sizes[1]

    def peer(stage, offset):
        axis, stride, size = stage
        digit = lax.rem(place[axis] // stride, size)
        other = lax.rem(digit + offset, size)
        return axis, digit, other, place[axis] + (other - digit) * stride

    copy_start = pltpu.make_async_copy(start_hbm, allv.at[earlier], in_sem.at[0])
    copy_coef = pltpu.make_async_copy(coef_hbm, coef_in, in_sem.at[1])
    copy_early = pltpu.make_async_copy(early_hbm, allv.at[pl.ds(0, earlier)], in_sem.at[2])
    copy_start.start()
    copy_coef.start()
    copy_early.start()

    halo_x[...] = jnp.zeros_like(halo_x)
    halo_z[...] = jnp.zeros_like(halo_z)
    send_z[...] = jnp.zeros_like(send_z)
    ee[...] = jnp.zeros_like(ee)

    barrier = pltpu.get_barrier_semaphore()
    expected = 0
    for stage in stages:
        for offset in range(1, stage[2]):
            axis, _, _, target = peer(stage, offset)
            pl.semaphore_signal(barrier, inc=1, device_id={axis: target}, device_id_type=MESH)
            expected += 1
    extra = [(axis, n) for axis, n in sizes if len(factors(n)) > 1]
    for axis, n in extra:
        for off in (-1, 1):
            there = jnp.logical_and(place[axis] + off >= 0, place[axis] + off < n)

            @pl.when(there)
            def _():
                pl.semaphore_signal(
                    barrier, inc=1, device_id={axis: place[axis] + off}, device_id_type=MESH
                )

    def halo_copy(step, kind, side):
        axis, n = (slab, sub)[kind]
        if kind == 0:
            src, dst = send_z.at[step, side], halo_z.at[step, side]
        else:
            src = allv.at[earlier + step, :, width - 1 if side == 0 else 0]
            dst = halo_x.at[step, side]
        target = place[axis] + (1 if side == 0 else -1)
        return pltpu.make_async_remote_copy(
            src_ref=src, dst_ref=dst,
            send_sem=halo_send.at[step, kind, side], recv_sem=halo_recv.at[step, kind, side],
            device_id={axis: target}, device_id_type=MESH,
        )

    def has(kind, side, sending):
        axis, n = (slab, sub)[kind]
        upward = (side == 0) == sending
        return place[axis] < n - 1 if upward else place[axis] > 0

    def pack(step):
        for e in range(comp):
            for x in range(width):
                row = 4 * e + x
                tile = allv.at[earlier + step, e, x]
                send_z[step, 0, row:row + 1, :] = tile[ROWS - 1:ROWS, :]
                send_z[step, 1, row:row + 1, :] = tile[0:1, :]

    def send(step):
        for kind in (0, 1):
            for side in (0, 1):
                @pl.when(has(kind, side, True))
                def _():
                    halo_copy(step, kind, side).start()

    copy_start.wait()
    pack(0)
    for axis, n in extra:
        for off in (-1, 1):
            there = jnp.logical_and(place[axis] + off >= 0, place[axis] + off < n)

            @pl.when(there)
            def _():
                pl.semaphore_wait(barrier, 1)
    pl.semaphore_wait(barrier, expected)
    send(0)

    copy_coef.wait()

    @pl.loop(0, comp)
    def _(c):
        for d in range(coef.shape[0]):
            coef[d, c] = coef_in[d, c].astype(jnp.float32)
        edge_coef[c] = jnp.zeros_like(edge_coef[c])
        for e in range(comp):
            for x in range(width):
                edge_coef[c, e, x:x + 1, :] = coef[1, c, e, x, 0:1, :]
                edge_coef[c, e, 4 + x:5 + x, :] = coef[2, c, e, x, ROWS - 1:ROWS, :]

    copy_early.wait()

    def self_products(c):
        part = side_by_side(allv[pl.ds(0, earlier), c])
        ee[...] += dot(part, part, nt=True)

    row3 = iota((width, ROWS, LANES), 1)
    lane3 = iota((width, ROWS, LANES), 2)
    row2 = iota((ROWS, LANES), 0)
    zero_tile = jnp.zeros((1, ROWS, LANES), jnp.float32)

    @pl.loop(0, depth)
    def _(step):
        acc = (1.0 - shifts_ref[step]) * allv[earlier + step]
        for e in range(comp):
            v = allv[earlier + step, e]
            near = [
                v,
                jnp.where(row3 > 0, pltpu.roll(v, 1, 1), 0.0),
                jnp.where(row3 < ROWS - 1, pltpu.roll(v, ROWS - 1, 1), 0.0),
                jnp.concatenate([zero_tile, v[:-1]], axis=0),
                jnp.concatenate([v[1:], zero_tile], axis=0),
                jnp.where(lane3 > 0, pltpu.roll(v, 1, 2), 0.0),
                jnp.where(lane3 < LANES - 1, pltpu.roll(v, LANES - 1, 2), 0.0),
            ]
            for d in range(len(near)):
                acc = acc + coef[d, :, e] * near[d][None]
        acc_ref[...] = acc

        @pl.loop(step * comp // depth, (step + 1) * comp // depth)
        def _(c):
            self_products(c)

        for kind in (0, 1):
            for side in (0, 1):
                @pl.when(has(kind, side, False))
                def _():
                    halo_copy(step, kind, side).wait_recv()

        edge = jnp.zeros((comp, ROWS, LANES), jnp.float32)
        low = jnp.zeros((comp, ROWS, LANES), jnp.float32)
        high = jnp.zeros((comp, ROWS, LANES), jnp.float32)
        for e in range(comp):
            base = ROWS * (e // 2)
            below = halo_z[step, 0, base:base + ROWS, :]
            above = halo_z[step, 1, base:base + ROWS, :]
            if e % 2 == 0:
                above = pltpu.roll(above, 4, 0)
            else:
                below = pltpu.roll(below, 4, 0)
            edge = edge + edge_coef[:, e] * jnp.where(row2 < 4, below, above)[None]
            low = low + coef[3, :, e, 0] * halo_x[step, 0, e][None]
            high = high + coef[4, :, e, width - 1] * halo_x[step, 1, e][None]
        for c in range(comp):
            for x in range(width):
                value = acc_ref[c, x]
                if x == 0:
                    value = value + low[c]
                if x == width - 1:
                    value = value + high[c]
                value = value + jnp.where(
                    row2 == 0, edge[c, x:x + 1, :],
                    jnp.where(row2 == ROWS - 1, edge[c, 4 + x:5 + x, :], 0.0),
                )
                allv[earlier + step + 1, c, x] = value

        @pl.when(step < depth - 1)
        def _():
            pack(step + 1)
            send(step + 1)

    total = earlier + block
    cross = jnp.zeros((block * ROWS, total * ROWS), jnp.float32)
    for c in range(comp):
        part = side_by_side(allv[:, c])
        cross = cross + dot(part[earlier * ROWS:], part, nt=True)

    def diagonal(value):
        r, q = iota(value.shape, 0), iota(value.shape, 1)
        return jnp.where((r & 7) == (q & 7), value, 0.0)

    wide = dot(diagonal(cross), onehot((total * ROWS, LANES), lambda r, q: (r >> 3) == q))
    mine[0] = dot(onehot((ROWS, block * ROWS), lambda r, q: (q >> 3) == r), wide)
    span = earlier * ROWS
    wide = dot(diagonal(ee[...]), onehot((span, LANES), lambda r, q: (r >> 3) == (q & 31)))
    wide = jnp.where((iota(wide.shape, 0) >> 6) == (iota(wide.shape, 1) >> 5), wide, 0.0)
    mine[1] = dot(onehot((ROWS, span), lambda r, q: ((q >> 3) & 7) == r), wide)

    for at, stage in enumerate(stages):
        size = stage[2]
        source = mine.at[pl.ds(2 * at, 2)]

        def move(offset, sending):
            axis, digit, other, target = peer(stage, offset)
            return pltpu.make_async_remote_copy(
                src_ref=source, dst_ref=gathered.at[at, digit],
                send_sem=red_send.at[at, other],
                recv_sem=red_recv.at[at, digit if sending else other],
                device_id={axis: target}, device_id_type=MESH,
            )

        for offset in range(1, size):
            move(offset, True).start()
        digit = peer(stage, 0)[1]
        gathered[at, digit] = source[...]
        for offset in range(1, size):
            move(offset, False).wait_recv()
        whole = gathered[at, 0]
        for other in range(1, size):
            whole = whole + gathered[at, other]
        mine[2 * at + 2:2 * at + 4] = whole
    sums = mine[2 * len(stages):2 * len(stages) + 2] * (1.0 / count)

    lane = iota((ROWS, LANES), 1)
    proj_t = jnp.where(lane < earlier, sums[0], 0.0)
    gram = pltpu.roll(sums[0], LANES - earlier, 1)[:, :ROWS]
    packed = sums[1]
    square = jnp.concatenate(
        [packed] + [pltpu.roll(packed, LANES - 32 * g, 1) for g in range(1, 4)], axis=0
    )
    sr, sl = iota(square.shape, 0), iota(square.shape, 1)
    square = jnp.where(sl < 32, square, 0.0) - jnp.where(sr == sl, 2.0, 0.0)
    gram = gram + dot(dot(proj_t[:, :32], square), proj_t, nt=True)

    upper = gram
    inverse = onehot((ROWS, ROWS), lambda r, q: r == q)
    r8 = iota((ROWS, ROWS), 0)
    q8 = iota((ROWS, ROWS), 1)
    for p in range(block):
        pivot = upper[p:p + 1, p:p + 1]
        scale = lax.rsqrt(pivot)
        scale = scale * (1.5 - 0.5 * pivot * scale * scale)
        column = upper[:, p:p + 1] * scale
        row_u, row_i = upper[p:p + 1, :] * scale, inverse[p:p + 1, :] * scale
        upper = jnp.where(r8 == p, row_u, jnp.where(r8 > p, upper - column * row_u, upper))
        inverse = jnp.where(r8 == p, row_i, jnp.where(r8 > p, inverse - column * row_i, inverse))
    tri_ref[...] = jnp.where(q8 >= r8, upper, 0.0)[:block, :block]
    proj_ref[...] = proj_t[:block, :earlier]

    pick = onehot((ROWS, LANES), lambda r, q: q == r + earlier)
    mix = dot(inverse, pick - proj_t)
    mix = dot(onehot((block * ROWS, ROWS), lambda r, q: (r >> 3) == q), mix)
    mix = diagonal(dot(mix, onehot((LANES, total * ROWS), lambda r, q: (q >> 3) == r)))
    for c in range(comp):
        out = dot(mix, side_by_side(allv[:, c]))
        for x in range(width):
            new_ref[:, c, x] = out[:, LANES * x:LANES * (x + 1)].reshape(block, ROWS, LANES)

    @pl.loop(0, depth)
    def _(step):
        for kind in (0, 1):
            for side in (0, 1):
                @pl.when(has(kind, side, True))
                def _():
                    halo_copy(step, kind, side).wait_send()

    for at, stage in enumerate(stages):
        for offset in range(1, stage[2]):
            axis, digit, other, target = peer(stage, offset)
            pltpu.make_async_remote_copy(
                src_ref=mine.at[pl.ds(2 * at, 2)], dst_ref=gathered.at[at, digit],
                send_sem=red_send.at[at, other], recv_sem=red_recv.at[at, digit],
                device_id={axis: target}, device_id_type=MESH,
            ).wait_send()


def body(sizes, coefficients, earlier, start, shifts):
    coefficients = jnp.transpose(coefficients, (0, 1, 2, 4, 3, 5))
    earlier = jnp.transpose(earlier, (0, 1, 3, 2, 4))
    start = jnp.transpose(start, (0, 2, 1, 3))
    depth, count = shifts.shape[0], earlier.shape[0]
    block = depth + 1
    kinds, comp, _, width, rows, lanes = coefficients.shape
    stages = stages_of(sizes)
    most = max(stage[2] for stage in stages)
    f32 = jnp.float32
    anywhere = pl.BlockSpec(memory_space=pl.ANY)
    vmem = pl.BlockSpec(memory_space=pltpu.VMEM)
    new, proj, tri = pl.pallas_call(
        functools.partial(kernel, sizes),
        out_shape=(
            jax.ShapeDtypeStruct((block, comp, width, rows, lanes), f32),
            jax.ShapeDtypeStruct((block, count), f32),
            jax.ShapeDtypeStruct((block, block), f32),
        ),
        in_specs=[anywhere, anywhere, anywhere, pl.BlockSpec(memory_space=pltpu.SMEM)],
        out_specs=(vmem, vmem, vmem),
        scratch_shapes=[
            pltpu.VMEM(coefficients.shape, coefficients.dtype),
            pltpu.VMEM(coefficients.shape, f32),
            pltpu.VMEM((comp, comp, rows, lanes), f32),
            pltpu.VMEM((count + block, comp, width, rows, lanes), f32),
            pltpu.VMEM((comp, width, rows, lanes), f32),
            pltpu.VMEM((depth, 2, comp, rows, lanes), f32),
            pltpu.VMEM((depth, 2, 4 * comp, lanes), f32),
            pltpu.VMEM((depth, 2, 4 * comp, lanes), f32),
            pltpu.VMEM((count * rows, count * rows), f32),
            pltpu.VMEM((2 * len(stages) + 2, rows, lanes), f32),
            pltpu.VMEM((len(stages), most, 2, rows, lanes), f32),
            pltpu.SemaphoreType.DMA((3,)),
            pltpu.SemaphoreType.DMA((depth, 2, 2)),
            pltpu.SemaphoreType.DMA((depth, 2, 2)),
            pltpu.SemaphoreType.DMA((len(stages), most)),
            pltpu.SemaphoreType.DMA((len(stages), most)),
        ],
        compiler_params=pltpu.CompilerParams(collective_id=0, has_side_effects=True),
        name="powers",
    )(coefficients, earlier, start, shifts)
    return jnp.transpose(new, (0, 1, 3, 2, 4)), proj.T, tri


def solution(mesh):
    sizes = (("slab", mesh.shape["slab"]), ("sub", mesh.shape["sub"]))
    placed = (
        P(None, None, None, "slab", "sub", None),
        P(None, None, "slab", "sub", None),
        P(None, "slab", "sub", None),
        P(),
    )
    return jax.shard_map(
        functools.partial(body, sizes),
        mesh=mesh,
        in_specs=placed,
        out_specs=(P(None, None, "slab", "sub", None), P(), P()),
        check_vma=False,
    )
```

time: 178 us -> 43.9 us (0.25)
  blocking collectives: 42.9 us -> 0 us
  Pallas kernels: 0 us -> 38.7 us
  starting transfers between devices: 37.9 us -> 0 us
  local copies, waits for them, and re-layouts: 32.4 us -> 4.34 us
  waiting for transfers between devices: 28 us -> 0 us
  other arithmetic: 21.6 us -> 0 us
  matrix products: 9.97 us -> 0 us
  between operations: 4.5 us -> 0.64 us
    psum x1 -> x0, blocking collectives: 42.9 us -> none  [body(): lax.psum((local_cross, local_self, local_earlier), ('slab', 'sub'))]
    pallas_call x0 -> x1, Pallas kernels: none -> 38.7 us  [body(): pl.pallas_call(functools.partial(kernel, sizes), out_shape=(jax.ShapeDtyp...]
    ppermute x14 -> x0, starting transfers between devices: 37.9 us -> none  [the longest x7 28.7 us: padded_2(): lax.ppermute(lax.slice_in_dim(block, block.shape[dim] - width, None, axis...]
    ppermute x14 -> x0, waiting for transfers between devices: 28 us -> none  [the longest x7 21.9 us: padded_2(): lax.ppermute(lax.slice_in_dim(block, block.shape[dim] - width, None, axis...]
    reduce_sum x5 -> x0, other arithmetic: 15.2 us -> none  [apply_padded(): jnp.sum(coefficients[coupling] * fields[coupling][None], axis=1)]
    dot_general x7 -> x0, matrix products: 9.22 us -> none  [the longest x1 2.88 us: body(): jnp.dot(projection.T, earlier_flat, precision=lax.Precision.HIGHEST)]
    another operation x18 -> x0, local copies, waits for them, and re-layouts: 8.1 us -> none  [body(): basis = jnp.stack(vectors)]
    slice x22 -> x0, local copies, waits for them, and re-layouts: 7.66 us -> none  [the longest x7 6.15 us: padded_2(): lax.slice_in_dim(block, block.shape[dim] - width, None, axis=dim)]
  transfers between devices with their start and end apart: 14 -> 0, of which waited for: 4 -> 0; matrix products, arithmetic and copies ran while one was open for 14% -> 0% of each run, Pallas kernels for 0% -> 0%
where the time goes in v1:
time: 43.9 us; the launch traced here: 43.7 us
  Pallas kernels  38.7 us (88%)
  local copies, waits for them, and re-layouts  4.34 us (10%)
  between operations  0.64 us (1%)
    pallas_call x1, Pallas kernels, body(): pl.pallas_call(functools.partial(kernel, sizes), out_shape=(jax.ShapeDtyp...  38.7 us
    unnamed x3, local copies, waits for them, and re-layouts  4.34 us

profile of v1, /device:TPU:0, one launch (start us, length us, event | category | flops | bytes accessed | tf_op | source)
XLA Modules:
  0.0 43.7 jit_solution(337268952377801028)
XLA Ops:
  0.6 38.7 %powers.1 = (f32[6,6,3,8,128]{4,3,2,1,0:T(8,128)}, f32[6,30]{1,0:T(8,128)}, f32[6,6]{1,0:T(8,128)}) custom-call(bf16[7,6,6,3,8,128]{5,4,3,2,1,0:T(8,128)(2,1)} %bitcast.6, f32[30,6,3,8,128]{4,3,2,1,0:T(8,128)} %bitcast.5, f32[6,3,8,128]{3,2,1,0:T(8,128)} %bitcast.8, f32[5]{0:T(128)} %shifts_ref.1), custom_call_target="tpu_custom_call" | custom-call | tf_op jit(solution)/shard_map/powers/pallas_call | solution.py:343
  39.4 1.8 %copy.10 = f32[6,6,8,3,128]{4,2,3,1,0:T(8,128)} copy(f32[6,6,8,3,128]{4,2,3,1,0:T(8,128)} %bitcast.7) | data formatting | bytes 884736
  41.2 1.3 %copy.11 = f32[30,6]{0,1:T(8,128)} copy(f32[30,6]{0,1:T(8,128)} %bitcast.9) | data formatting | bytes 1440
  42.4 1.3 %copy.12 = f32[6,6]{1,0:T(8,128)} copy(f32[6,6]{1,0:T(8,128)} %get-tuple-element.14) | data formatting | bytes 288

commit v2 on v1

--- a/solution.py
+++ b/solution.py
@@ -48,6 +48,34 @@
     return found
 
 
+def diagonal(value):
+    r, q = iota(value.shape, 0), iota(value.shape, 1)
+    return jnp.where((r & 7) == (q & 7), value, 0.0)
+
+
+def split(value):
+    first = value.astype(jnp.bfloat16)
+    left = value - first.astype(jnp.float32)
+    second = left.astype(jnp.bfloat16)
+    third = (left - second.astype(jnp.float32)).astype(jnp.bfloat16)
+    return [first, second, third]
+
+
+def dot_pieces(a, b, nt=False):
+    found = None
+    rows = a[0].shape[0]
+    for at in (2, 1, 0):
+        left = jnp.concatenate(a[: 3 - at], axis=0)
+        part = lax.dot_general(
+            left, b[at], (((1,), (1 if nt else 0,)), ((), ())),
+            preferred_element_type=jnp.float32,
+        )
+        for i in reversed(range(3 - at)):
+            piece = part[i * rows:(i + 1) * rows]
+            found = piece if found is None else found + piece
+    return found
+
+
 def side_by_side(value):
     count, width = value.shape[0], value.shape[1]
     return jnp.concatenate(
@@ -56,8 +84,9 @@
 
 
 def kernel(
-    sizes, coef_hbm, early_hbm, start_hbm, shifts_ref, new_ref, proj_ref, tri_ref,
-    coef_in, coef, edge_coef, allv, acc_ref, halo_x, halo_z, send_z, ee, mine, gathered,
+    sizes, coef_hbm, early_hbm, start_hbm, shifts_ref, new_ref, small_ref,
+    coef_in, coef, edge_coef, allv, pieces, acc_ref, halo_x, halo_z, send_z, ee, sums_ref,
+    mine, gathered,
     in_sem, halo_send, halo_recv, red_send, red_recv,
 ):
     depth = shifts_ref.shape[0]
@@ -85,6 +114,10 @@
     halo_z[...] = jnp.zeros_like(halo_z)
     send_z[...] = jnp.zeros_like(send_z)
     ee[...] = jnp.zeros_like(ee)
+    mine[0] = jnp.zeros_like(mine[0])
+    sums_ref[...] = jnp.zeros_like(sums_ref)
+    for k in range(1, block):
+        allv[earlier + k] = jnp.zeros_like(allv[earlier + k])
 
     barrier = pltpu.get_barrier_semaphore()
     expected = 0
@@ -165,8 +198,26 @@
     copy_early.wait()
 
     def self_products(c):
-        part = side_by_side(allv[pl.ds(0, earlier), c])
-        ee[...] += dot(part, part, nt=True)
+        parts = split(side_by_side(allv[pl.ds(0, earlier), c]))
+        for at, part in enumerate(parts):
+            pieces[at, c] = part
+        ee[...] += dot_pieces(parts, [parts[0], parts[1], parts[2]], nt=True)
+
+    def cross_products(k):
+        total, group = earlier + block, 6
+        w = allv[earlier + k]
+        for low in range(0, total, group):
+            high = min(low + group, total)
+            part = jnp.sum(w[None] * allv[low:high], axis=(1, 2))
+            sums_ref[low:high, :] = jnp.sum(part, axis=1)
+        line = dot(jnp.ones((ROWS, LANES), jnp.float32), sums_ref[...], nt=True)
+        mine[0, pl.ds(k, 1), :] = line[0:1]
+
+    def self_finish():
+        span = earlier * ROWS
+        wide = dot(diagonal(ee[...]), onehot((span, LANES), lambda r, q: (r >> 3) == (q & 31)))
+        wide = jnp.where((iota(wide.shape, 0) >> 6) == (iota(wide.shape, 1) >> 5), wide, 0.0)
+        mine[1] = dot(onehot((ROWS, span), lambda r, q: ((q >> 3) & 7) == r), wide)
 
     row3 = iota((width, ROWS, LANES), 1)
     lane3 = iota((width, ROWS, LANES), 2)
@@ -191,9 +242,17 @@
                 acc = acc + coef[d, :, e] * near[d][None]
         acc_ref[...] = acc
 
-        @pl.loop(step * comp // depth, (step + 1) * comp // depth)
+        cross_products(step)
+
+        @pl.loop(
+            step * comp // (depth - 1), jnp.minimum((step + 1) * comp // (depth - 1), comp)
+        )
         def _(c):
             self_products(c)
+
+        @pl.when(step == depth - 1)
+        def _():
+            self_finish()
 
         for kind in (0, 1):
             for side in (0, 1):
@@ -233,22 +292,8 @@
             pack(step + 1)
             send(step + 1)
 
+    cross_products(depth)
     total = earlier + block
-    cross = jnp.zeros((block * ROWS, total * ROWS), jnp.float32)
-    for c in range(comp):
-        part = side_by_side(allv[:, c])
-        cross = cross + dot(part[earlier * ROWS:], part, nt=True)
-
-    def diagonal(value):
-        r, q = iota(value.shape, 0), iota(value.shape, 1)
-        return jnp.where((r & 7) == (q & 7), value, 0.0)
-
-    wide = dot(diagonal(cross), onehot((total * ROWS, LANES), lambda r, q: (r >> 3) == q))
-    mine[0] = dot(onehot((ROWS, block * ROWS), lambda r, q: (q >> 3) == r), wide)
-    span = earlier * ROWS
-    wide = dot(diagonal(ee[...]), onehot((span, LANES), lambda r, q: (r >> 3) == (q & 31)))
-    wide = jnp.where((iota(wide.shape, 0) >> 6) == (iota(wide.shape, 1) >> 5), wide, 0.0)
-    mine[1] = dot(onehot((ROWS, span), lambda r, q: ((q >> 3) & 7) == r), wide)
 
     for at, stage in enumerate(stages):
         size = stage[2]
@@ -275,16 +320,19 @@
         mine[2 * at + 2:2 * at + 4] = whole
     sums = mine[2 * len(stages):2 * len(stages) + 2] * (1.0 / count)
 
-    lane = iota((ROWS, LANES), 1)
+    row, lane = iota((ROWS, LANES), 0), iota((ROWS, LANES), 1)
     proj_t = jnp.where(lane < earlier, sums[0], 0.0)
-    gram = pltpu.roll(sums[0], LANES - earlier, 1)[:, :ROWS]
+    known = jnp.where(lane < earlier + row, sums[0], 0.0)
+    pick = onehot((ROWS, LANES), lambda r, q: q == r + earlier)
+    gram = jnp.where(lane <= earlier + row, sums[0], 0.0)
+    gram = pltpu.roll(gram, LANES - earlier, 1)[:, :ROWS]
     packed = sums[1]
     square = jnp.concatenate(
         [packed] + [pltpu.roll(packed, LANES - 32 * g, 1) for g in range(1, 4)], axis=0
     )
     sr, sl = iota(square.shape, 0), iota(square.shape, 1)
     square = jnp.where(sl < 32, square, 0.0) - jnp.where(sr == sl, 2.0, 0.0)
-    gram = gram + dot(dot(proj_t[:, :32], square), proj_t, nt=True)
+    gram = gram + dot(dot(proj_t[:, :32], square) + pick, known, nt=True)
 
     upper = gram
     inverse = onehot((ROWS, ROWS), lambda r, q: r == q)
@@ -298,17 +346,30 @@
         row_u, row_i = upper[p:p + 1, :] * scale, inverse[p:p + 1, :] * scale
         upper = jnp.where(r8 == p, row_u, jnp.where(r8 > p, upper - column * row_u, upper))
         inverse = jnp.where(r8 == p, row_i, jnp.where(r8 > p, inverse - column * row_i, inverse))
-    tri_ref[...] = jnp.where(q8 >= r8, upper, 0.0)[:block, :block]
-    proj_ref[...] = proj_t[:block, :earlier]
-
-    pick = onehot((ROWS, LANES), lambda r, q: q == r + earlier)
+    small_ref[0:ROWS, :] = proj_t
+    small_ref[ROWS:2 * ROWS, 0:ROWS] = jnp.where(q8 >= r8, upper, 0.0)
+
     mix = dot(inverse, pick - proj_t)
-    mix = dot(onehot((block * ROWS, ROWS), lambda r, q: (r >> 3) == q), mix)
-    mix = diagonal(dot(mix, onehot((LANES, total * ROWS), lambda r, q: (q >> 3) == r)))
+    tall = dot(onehot((block * ROWS, ROWS), lambda r, q: (r >> 3) == q), mix)
+    span = earlier * ROWS
+    mix = split(diagonal(dot(tall, onehot((LANES, span), lambda r, q: (q >> 3) == r))))
+    weights = [
+        [
+            jnp.broadcast_to(
+                tall[k * ROWS:(k + 1) * ROWS, earlier + i:earlier + i + 1], (ROWS, LANES)
+            )
+            for i in range(k + 1)
+        ]
+        for k in range(block)
+    ]
     for c in range(comp):
-        out = dot(mix, side_by_side(allv[:, c]))
+        out = dot_pieces(mix, [pieces[at, c] for at in range(3)])
         for x in range(width):
-            new_ref[:, c, x] = out[:, LANES * x:LANES * (x + 1)].reshape(block, ROWS, LANES)
+            for k in range(block):
+                value = out[k * ROWS:(k + 1) * ROWS, LANES * x:LANES * (x + 1)]
+                for i in range(k + 1):
+                    value = value + weights[k][i] * allv[earlier + i, c, x]
+                new_ref[k, c, x] = value
 
     @pl.loop(0, depth)
     def _(step):
@@ -326,6 +387,12 @@
                 send_sem=red_send.at[at, other], recv_sem=red_recv.at[at, digit],
                 device_id={axis: target}, device_id_type=MESH,
             ).wait_send()
+
+
+def hand_over(rows, new_in, small, new_out, proj_out, tri_out):
+    new_out[...] = new_in[...]
+    proj_out[...] = small[: proj_out.shape[0], : proj_out.shape[1]]
+    tri_out[...] = small[rows:rows + tri_out.shape[0], : tri_out.shape[1]]
 
 
 def body(sizes, coefficients, earlier, start, shifts):
@@ -340,25 +407,26 @@
     f32 = jnp.float32
     anywhere = pl.BlockSpec(memory_space=pl.ANY)
     vmem = pl.BlockSpec(memory_space=pltpu.VMEM)
-    new, proj, tri = pl.pallas_call(
+    new, small = pl.pallas_call(
         functools.partial(kernel, sizes),
         out_shape=(
             jax.ShapeDtypeStruct((block, comp, width, rows, lanes), f32),
-            jax.ShapeDtypeStruct((block, count), f32),
-            jax.ShapeDtypeStruct((block, block), f32),
+            jax.ShapeDtypeStruct((2 * rows, lanes), f32),
         ),
         in_specs=[anywhere, anywhere, anywhere, pl.BlockSpec(memory_space=pltpu.SMEM)],
-        out_specs=(vmem, vmem, vmem),
+        out_specs=(vmem, vmem),
         scratch_shapes=[
             pltpu.VMEM(coefficients.shape, coefficients.dtype),
             pltpu.VMEM(coefficients.shape, f32),
             pltpu.VMEM((comp, comp, rows, lanes), f32),
             pltpu.VMEM((count + block, comp, width, rows, lanes), f32),
+            pltpu.VMEM((3, comp, count * rows, width * lanes), jnp.bfloat16),
             pltpu.VMEM((comp, width, rows, lanes), f32),
             pltpu.VMEM((depth, 2, comp, rows, lanes), f32),
             pltpu.VMEM((depth, 2, 4 * comp, lanes), f32),
             pltpu.VMEM((depth, 2, 4 * comp, lanes), f32),
             pltpu.VMEM((count * rows, count * rows), f32),
+            pltpu.VMEM((lanes, lanes), f32),
             pltpu.VMEM((2 * len(stages) + 2, rows, lanes), f32),
             pltpu.VMEM((len(stages), most, 2, rows, lanes), f32),
             pltpu.SemaphoreType.DMA((3,)),
@@ -370,6 +438,17 @@
         compiler_params=pltpu.CompilerParams(collective_id=0, has_side_effects=True),
         name="powers",
     )(coefficients, earlier, start, shifts)
+    new, proj, tri = pl.pallas_call(
+        functools.partial(hand_over, rows),
+        out_shape=(
+            jax.ShapeDtypeStruct(new.shape, f32),
+            jax.ShapeDtypeStruct((block, count), f32),
+            jax.ShapeDtypeStruct((block, block), f32),
+        ),
+        in_specs=[vmem, vmem],
+        out_specs=(vmem, vmem, vmem),
+        name="hand_over",
+    )(new, small)
     return jnp.transpose(new, (0, 1, 3, 2, 4)), proj.T, tri
 
 

time: 43.9 us -> 35.6 us (0.81)
  local copies, waits for them, and re-layouts: 4.34 us -> 0 us
  Pallas kernels: 38.7 us -> 34.8 us
    pallas_call x1, Pallas kernels: 38.7 us -> 33 us  [body(): pl.pallas_call(functools.partial(kernel, sizes), out_shape=(jax.ShapeDtyp...]
    unnamed x3 -> x0, local copies, waits for them, and re-layouts: 4.34 us -> none
    pallas_call x0 -> x1, Pallas kernels: none -> 1.81 us  [body(): pl.pallas_call(functools.partial(hand_over, rows), out_shape=(jax.ShapeDt...]
where the time goes in v2:
time: 35.6 us; the launch traced here: 35.5 us
  Pallas kernels  34.8 us (98%)
  between operations  0.64 us (2%)
    pallas_call x1, Pallas kernels, body(): pl.pallas_call(functools.partial(kernel, sizes), out_shape=(jax.ShapeDtyp...  33 us
    pallas_call x1, Pallas kernels, body(): pl.pallas_call(functools.partial(hand_over, rows), out_shape=(jax.ShapeDt...  1.81 us

profile of v2, /device:TPU:0, one launch (start us, length us, event | category | flops | bytes accessed | tf_op | source)
XLA Modules:
  0.0 35.5 jit_solution(11164209650053163224)
XLA Ops:
  0.6 33.0 %powers.1 = (f32[6,6,3,8,128]{4,3,2,1,0:T(8,128)}, f32[16,128]{1,0:T(8,128)}) custom-call(bf16[7,6,6,3,8,128]{5,4,3,2,1,0:T(8,128)(2,1)} %bitcast.6, f32[30,6,3,8,128]{4,3,2,1,0:T(8,128)} %bitcast.5, f32[6,3,8,128]{3,2,1,0:T(8,128)} %bitcast.7, f32[5]{0:T(128)} %shifts_ref.1), custom_call_target="tpu_custom_call" | custom-call | tf_op jit(solution)/shard_map/powers/pallas_call | solution.py:410
  33.7 1.8 %hand_over.1 = (f32[6,6,3,8,128]{4,3,2,1,0:T(8,128)}, f32[6,30]{1,0:T(8,128)}, f32[6,6]{1,0:T(8,128)}) custom-call(f32[6,6,3,8,128]{4,3,2,1,0:T(8,128)} %get-tuple-element.8.new_in, f32[16,128]{1,0:T(8,128)} %get-tuple-element.9.small), custom_call_target="tpu_custom_call" | custom-call | tf_op jit(solution)/shard_map/hand_over/pallas_call | solution.py:441
